TPU v7x, 32 devices: a whole 2x2x4 slice. The times are simulated.
32 devices in a mesh: groups: 2 (over y), ctx: 4 (over z), tp: 4 (over x, core).
Axes of the slice: x: 2, y: 2, z: 4, core: 2. Of those that a mesh axis runs over, the one named last changes fastest.
Arguments:
- streams: bfloat16 [3, 1024, 8192], P(None, ('groups', 'ctx'), 'tp'), parts along dimension 1, may hold values from -6 to 6
- short_filter: float32 [3, 3, 8192], P(None, None, 'tp'), may hold values from -3 to 3
- decay_rate: float32 [8192, 16], P('tp'), may hold values from 0 to 1
- residue: float32 [8192, 16], P('tp'), may hold values from -0.2 to 0.2
- skip_gain: float32 [8192], P('tp'), may hold values from -4 to 4
- lengths: int32 [4], P('groups'), parts along dimension 0, may hold values from 1 to 448, 512 in all
- queries: bfloat16 [1024, 8192], P(('groups', 'ctx'), 'tp'), parts along dimension 0, may hold values from -8 to 8
- keys: bfloat16 [1024, 8192], P(('groups', 'ctx'), 'tp'), parts along dimension 0, may hold values from -8 to 8
Outputs:
- hyena_out: bfloat16 [1024, 8192], P(('groups', 'ctx'), 'tp'), parts along dimension 0
- attended: bfloat16 [1024, 8192], P(('groups', 'ctx'), 'tp'), parts along dimension 0
There are 2 independent parts, one for each index of `groups`. A program takes and returns all parts, laid end to end along the dimension named above; an argument that names none is the same for every part. Nothing has to cross between parts.
Inputs may be any that keep to these rules, and one draw needn't show every extreme that they name: The requests fill the group in order, their lengths sum to 512, and the longest has at most 448 tokens.
All inputs are finite; a program needn't handle non-finite values.
Results may differ from a plain program's by a relative error of at most 0.01.
Values may be sent and summed in bfloat16 or wider, within the bound.
No kernel may reach another device: no remote copies, remote signals or barrier semaphores. Data moves between devices by JAX's collectives and lax.ppermute only.
A program may use at most 128 MiB of HBM per device.

v0:
```python
import functools
import math

import jax
import jax.numpy as jnp
from jax import lax
from jax.experimental import pallas as pl
from jax.experimental.pallas import tpu as pltpu
from jax.sharding import PartitionSpec as P


HEAD_DIM = 128
SHORT = 3
LANES = 128
NEG = -1e30


SMEM = pl.BlockSpec(memory_space=pltpu.SMEM)
VMEM = pl.BlockSpec(memory_space=pltpu.VMEM)
HBM = pl.BlockSpec(memory_space=pltpu.HBM)
SLOT = 32


def ends_of(lengths_ref):
    ends, total = [], jnp.int32(0)
    for r in range(lengths_ref.shape[0]):
        total = total + lengths_ref[r]
        ends.append(total)
    return ends


def start_of(place, ends):
    start = jnp.zeros_like(place)
    for end in ends:
        start = jnp.where(place >= end, end, start)
    return start


def end_of(place, ends):
    stop = ends[-1]
    for end in reversed(ends):
        stop = jnp.where(place < end, end, stop)
    return stop


def call(body, out, n_in, n_smem=1, scratch=(), flops=10**7, moved=4 * 10**6, space=VMEM):
    return pl.pallas_call(
        body,
        out_shape=out,
        in_specs=[SMEM] * n_smem + [space] * (n_in - n_smem),
        out_specs=jax.tree.map(lambda _: VMEM, out),
        scratch_shapes=list(scratch),
        compiler_params=pltpu.CompilerParams(vmem_limit_bytes=16 << 20),
        cost_estimate=pl.CostEstimate(flops=flops, bytes_accessed=moved, transcendentals=0),
    )


def hyena_local(lengths_ref, streams_ref, rim_ref, taps_ref, decay_ref, residue_ref, skip_ref,
                gate_ref, long_ref, state_ref, step_ref, block_ref, low_ref, high_ref,
                mixed_ref, gain_ref, final_ref):
    rows, width = gate_ref.shape
    modes = decay_ref.shape[0]
    tiles = width // LANES
    half = width // 2
    index = lax.axis_index("ctx")
    first = index * rows
    ends = ends_of(lengths_ref)

    row = lax.broadcasted_iota(jnp.int32, (rows, LANES), 0)
    place = row + first
    start = start_of(place, ends)
    inside = [None] + [(place - i >= start).astype(jnp.float32) for i in range(1, SHORT)]

    for j in range(tiles):
        lanes = slice(j * LANES, (j + 1) * LANES)
        filtered = []
        for s in range(3):
            x = streams_ref[s, :, lanes].astype(jnp.float32)
            rim = rim_ref[s, :, lanes].astype(jnp.float32)
            total = taps_ref[0, s : s + 1, lanes] * x
            for i in range(1, SHORT):
                moved = pltpu.roll(x, i, 0)
                for k in range(i):
                    moved = jnp.where(row == k, rim[SHORT - 1 - i + k : SHORT - i + k, :], moved)
                total = total + taps_ref[i, s : s + 1, lanes] * moved * inside[i]
            filtered.append(total)
        gate_ref[:, lanes] = filtered[0]
        mixed_ref[pl.ds(j, rows, stride=tiles), :] = filtered[1] * filtered[2]
        rate = decay_ref[:, lanes]
        step_ref[pl.ds(j, modes, stride=tiles), :] = jnp.exp(-rate)
        block_ref[pl.ds(j, modes, stride=tiles), :] = jnp.exp(-rate * rows)
        gain_ref[pl.ds(j, modes, stride=tiles), :] = residue_ref[:, lanes]

    for h in range(tiles // 8):
        decay = [step_ref[m * tiles + h * 8 : m * tiles + h * 8 + 8, :] for m in range(modes)]
        gain = [gain_ref[m * tiles + h * 8 : m * tiles + h * 8 + 8, :] for m in range(modes)]
        skip = skip_ref[h * 8 : h * 8 + 8, :]

        def advance(t, state):
            at = pl.ds(pl.multiple_of(t * tiles + h * 8, 8), 8)
            x = mixed_ref[at, :]
            state = tuple(s * d + g * x for s, d, g in zip(state, decay, gain))
            terms = list(state) + [skip * x]
            while len(terms) > 1:
                terms = [a + b for a, b in zip(terms[::2], terms[1::2])] + (
                    [terms[-1]] if len(terms) % 2 else []
                )
            long_ref[at, :] = terms[0]
            return state

        low = jnp.int32(0)
        for end in ends:
            high = jnp.clip(end - first, 0, rows)
            low_row = low

            def four(g, state, low_row=low_row):
                for u in range(4):
                    state = advance(low_row + g * 4 + u, state)
                return state

            groups = lax.shift_right_logical(high - low_row, 2)
            state = tuple(jnp.zeros((8, LANES), jnp.float32) for _ in range(modes))
            state = lax.fori_loop(0, groups, four, state)
            state = lax.fori_loop(low_row + groups * 4, high, advance, state)

            @pl.when((low_row < high) & (high == rows))
            def _(state=state):
                for m in range(modes):
                    final_ref[m * tiles + h * 8 : m * tiles + h * 8 + 8, :] = state[m]

            low = high
    state_ref[...] = final_ref[...].astype(state_ref.dtype)

    @pl.when(index == 0)
    def _():
        for j in range(tiles):
            lanes = slice(j * LANES, (j + 1) * LANES)
            value = gate_ref[:, lanes] * long_ref[pl.ds(j, rows, stride=tiles), :]
            out, at = (low_ref, j) if j * LANES < half else (high_ref, j - tiles // 2)
            out[:, at * LANES : (at + 1) * LANES] = value.astype(out.dtype)


def hyena_cross(hops, lengths_ref, step_ref, block_ref, long_ref, gate_ref, *refs):
    parts = refs[: len(hops)]
    value_ref, *halves, cross_ref = refs[len(hops) :]
    rows, width = gate_ref.shape
    tiles = width // LANES
    modes = step_ref.shape[0] // tiles
    index = lax.axis_index("ctx")
    first = index * rows
    ends = ends_of(lengths_ref)
    start = start_of(first - 1, ends)
    count = jnp.where(index > 0, jnp.clip(end_of(first - 1, ends) - first, 0, rows), 0)
    keeps = [
        ((first - 1 - hop * rows >= start) & (index > hop)).astype(jnp.float32) for hop in hops
    ]

    @pl.when(count > 0)
    def _():
        for h in range(tiles // 8):
            decay, incoming = [], []
            for m in range(modes):
                at = slice(m * tiles + h * 8, m * tiles + h * 8 + 8)
                decay.append(step_ref[at, :])
                total, factor = None, None
                for hop, keep, part in zip(hops, keeps, parts):
                    term = part[at, :].astype(jnp.float32) * keep
                    if hop:
                        factor = block_ref[at, :] if factor is None else factor * block_ref[at, :]
                        term = term * factor
                    total = term if total is None else total + term
                incoming.append(total)

            def advance(t, state):
                at = pl.ds(pl.multiple_of(t * tiles + h * 8, 8), 8)
                state = tuple(s * d for s, d in zip(state, decay))
                terms = list(state)
                while len(terms) > 1:
                    terms = [a + b for a, b in zip(terms[::2], terms[1::2])] + (
                        [terms[-1]] if len(terms) % 2 else []
                    )
                cross_ref[at, :] = terms[0]
                return state

            def four(g, state):
                for u in range(4):
                    state = advance(g * 4 + u, state)
                return state

            groups = lax.shift_right_logical(count, 2)
            state = lax.fori_loop(0, groups, four, tuple(incoming))
            lax.fori_loop(groups * 4, count, advance, state)

    row = lax.broadcasted_iota(jnp.int32, (rows, LANES), 0)
    reached = row < count
    for j in range(tiles):
        lanes = slice(j * LANES, (j + 1) * LANES)
        every = pl.ds(j, rows, stride=tiles)
        long = long_ref[every, :] + jnp.where(reached, cross_ref[every, :], 0.0)
        value_ref[:, lanes] = (gate_ref[:, lanes] * long).astype(value_ref.dtype)

    if halves:
        near_ref, other_ref = halves
        odd = index % 2 == 1
        copy_half(value_ref, near_ref, odd)
        copy_half(value_ref, other_ref, jnp.logical_not(odd))


def copy_half(source_ref, target_ref, lower):
    half = target_ref.shape[1]

    @pl.when(lower)
    def _():
        target_ref[...] = source_ref[:, :half]

    @pl.when(jnp.logical_not(lower))
    def _():
        target_ref[...] = source_ref[:, half:]


def pack(streams_ref, queries_ref, keys_ref, rim_ref, q_near, q_far, k_near, k_far, tail_ref, sems):
    reach_back = SHORT - 1
    rows, half = q_far.shape
    tail = tail_ref.shape[1]
    even = 1 - lax.axis_index("ctx") % 2
    near = pl.ds(pl.multiple_of(even * half, half), half)
    copies = [
        pltpu.make_async_copy(source, target, sems.at[i])
        for i, (source, target) in enumerate((
            (streams_ref.at[:, rows - tail :, :], tail_ref),
            (keys_ref.at[:, near], k_near),
            (keys_ref.at[:, :half], k_far),
            (queries_ref.at[:, near], q_near),
            (queries_ref.at[:, half:], q_far),
        ))
    ]
    for copy in copies:
        copy.start()
    copies[0].wait()
    rim_ref[...] = tail_ref[:, tail - reach_back :, :]
    for copy in copies[1:]:
        copy.wait()


def biases(query_block, key_blocks, rows, ends):
    place = query_block * rows + lax.broadcasted_iota(jnp.int32, (rows, rows), 0)
    start = start_of(place, ends)
    out = []
    for block in key_blocks:
        key = block * rows + lax.broadcasted_iota(jnp.int32, (rows, rows), 1)
        out.append(jnp.where((key >= start) & (key <= place), 0.0, NEG))
    return out


def one_head(query, pairs, bias):
    scale = 1.0 / math.sqrt(HEAD_DIM)
    base2 = scale * math.log2(math.e)
    dims = (((1,), (1,)), ((), ()))
    scores = [
        lax.dot_general(query, key, dims, preferred_element_type=jnp.float32) + b
        for (key, _), b in zip(pairs, bias)
    ]
    top = scores[0]
    for s in scores[1:]:
        top = jnp.maximum(top, s)
    top = jnp.max(top, axis=1, keepdims=True)
    weights = [jnp.exp2((s - top) * base2) for s in scores]
    total = weights[0]
    for w in weights[1:]:
        total = total + w
    total = jnp.sum(total, axis=1, keepdims=True)
    summed = None
    for w, (_, value) in zip(weights, pairs):
        part = jnp.dot(w.astype(jnp.bfloat16), value, preferred_element_type=jnp.float32)
        summed = part if summed is None else summed + part
    return summed / total, top * scale + jnp.log(total)


def cut(ref, h):
    return ref[:, h * HEAD_DIM : (h + 1) * HEAD_DIM]


def split3(x):
    a = x.astype(jnp.bfloat16)
    rest = x - a.astype(jnp.float32)
    b = rest.astype(jnp.bfloat16)
    c = (rest - b.astype(jnp.float32)).astype(jnp.bfloat16)
    return a, b, c


def attend(query_block, query_ref, query_at, sources, rows, count, ends, write):
    bias = biases(query_block, [block for block, _, _, _ in sources], rows, ends)
    for h in range(count):
        pairs = [(cut(keys, at + h), cut(values, h)) for _, keys, at, values in sources]
        write(h, *one_head(cut(query_ref, query_at + h), pairs, bias))


def serve(query_block, query_ref, sources, ends, out_ref):
    rows, half = query_ref.shape
    lane = lax.broadcasted_iota(jnp.int32, (rows, LANES), 1)
    stats = [jnp.zeros((rows, LANES), jnp.float32)]

    def write(h, mean, log_total):
        out_ref[:, h * HEAD_DIM : (h + 1) * HEAD_DIM] = mean.astype(out_ref.dtype)
        for k, piece in enumerate(split3(log_total)):
            stats[0] = jnp.where(lane == SLOT * k + h, piece.astype(jnp.float32), stats[0])

    attend(query_block, query_ref, 0, sources, rows, half // HEAD_DIM, ends, write)
    out_ref[:, half:] = stats[0].astype(out_ref.dtype)


def hub_far(lengths_ref, q2_ref, key_ref, other_ref, k1_ref, va_ref, far_ref):
    count = q2_ref.shape[1] // HEAD_DIM

    @pl.when(lax.axis_index("ctx") == 1)
    def _():
        sources = [(1, key_ref, count, other_ref), (0, k1_ref, 0, va_ref)]
        serve(3, q2_ref, sources, ends_of(lengths_ref), far_ref)


def hub_near(lengths_ref, q1_ref, key_ref, other_ref, k1_ref, va_ref, vb_ref, k2_ref, v2_ref,
             near_ref):
    count = q1_ref.shape[1] // HEAD_DIM
    index = lax.axis_index("ctx")
    ends = ends_of(lengths_ref)

    @pl.when(index == 0)
    def _():
        serve(1, q1_ref, [(0, key_ref, 0, other_ref)], ends, near_ref)

    @pl.when(index == 1)
    def _():
        sources = [(1, key_ref, count, other_ref), (0, k1_ref, 0, va_ref)]
        serve(2, q1_ref, sources, ends, near_ref)

    @pl.when(index == 2)
    def _():
        sources = [(2, key_ref, 0, other_ref), (1, k1_ref, 0, vb_ref), (0, k2_ref, 0, v2_ref)]
        serve(3, q1_ref, sources, ends, near_ref)


def own_half(query_ref, key_ref, mean_ref, stat_ref, ends, base, values, more=()):
    rows, width = query_ref.shape
    index = lax.axis_index("ctx")
    lane = lax.broadcasted_iota(jnp.int32, (rows, LANES), 1)
    stats = [jnp.zeros((rows, LANES), jnp.float32)]

    def write(h, mean, log_total):
        mean_ref[:, (base + h) * HEAD_DIM : (base + h + 1) * HEAD_DIM] = mean
        stats[0] = jnp.where(lane == h, log_total, stats[0])

    sources = [(index, key_ref, base, values), *more]
    attend(index, query_ref, base, sources, rows, width // HEAD_DIM // 2, ends, write)
    stat_ref[:, (LANES if base else 0) : (2 * LANES if base else LANES)] = stats[0]


def own_early(lengths_ref, query_ref, key_ref, near_ref, other_ref, mean_ref, stat_ref):
    count = query_ref.shape[1] // HEAD_DIM // 2
    index = lax.axis_index("ctx")
    run = functools.partial(
        own_half, query_ref, key_ref, mean_ref, stat_ref, ends_of(lengths_ref)
    )

    @pl.when(index == 0)
    def _():
        run(0, other_ref)

    @pl.when(index == 3)
    def _():
        run(0, near_ref)

    @pl.when(index % 2 == 0)
    def _():
        run(count, near_ref)


def own_late(lengths_ref, query_ref, key_ref, near_ref, other_ref, k1_ref, va_ref, vb_ref, k2_ref,
             v2_ref, mean_ref, stat_ref):
    count = query_ref.shape[1] // HEAD_DIM // 2
    index = lax.axis_index("ctx")
    run = functools.partial(
        own_half, query_ref, key_ref, mean_ref, stat_ref, ends_of(lengths_ref)
    )

    @pl.when(index == 1)
    def _():
        run(0, near_ref)
        run(count, other_ref, [(0, k1_ref, 0, va_ref)])

    @pl.when(index == 2)
    def _():
        run(0, other_ref, [(1, k1_ref, 0, vb_ref), (0, k2_ref, 0, v2_ref)])

    @pl.when(index == 3)
    def _():
        run(count, other_ref, [(2, k1_ref, 0, vb_ref)])


def merge(early_ref, early_stat, late_ref, late_stat, near_ref, far_ref, out_ref):
    _, width = early_ref.shape
    half = width // 2
    count = half // HEAD_DIM
    index = lax.axis_index("ctx")

    def join(base, mean_ref, stat_ref, other_ref):
        here = stat_ref[:, (LANES if base else 0) : (2 * LANES if base else LANES)]
        there = other_ref[:, half:].astype(jnp.float32)
        there = there + pltpu.roll(there, LANES - SLOT, 1) + pltpu.roll(there, LANES - 2 * SLOT, 1)
        top = jnp.maximum(here, there)
        a, b = jnp.exp(here - top), jnp.exp(there - top)
        norm = 1.0 / (a + b)
        a, b = a * norm, b * norm
        for h in range(count):
            at = slice((h + base) * HEAD_DIM, (h + base + 1) * HEAD_DIM)
            other = cut(other_ref, h).astype(jnp.float32)
            out_ref[:, at] = (
                mean_ref[:, at] * a[:, h : h + 1] + other * b[:, h : h + 1]
            ).astype(out_ref.dtype)

    def keep(base, mean_ref):
        at = slice(base * HEAD_DIM, (base + count) * HEAD_DIM)
        out_ref[:, at] = mean_ref[:, at].astype(out_ref.dtype)

    @pl.when(index == 0)
    def _():
        keep(0, early_ref)
        keep(count, early_ref)

    @pl.when(index == 1)
    def _():
        join(0, late_ref, late_stat, near_ref)
        keep(count, late_ref)

    @pl.when(index == 2)
    def _():
        keep(0, late_ref)
        join(count, early_ref, early_stat, near_ref)

    @pl.when(index == 3)
    def _():
        join(0, early_ref, early_stat, near_ref)
        join(count, late_ref, late_stat, far_ref)


def doc_of(places, ends):
    return jnp.sum((places[:, None] >= ends[None, :]).astype(jnp.int32), axis=1)


def gathered_attention(lengths, queries, keys, values):
    rows, width = queries.shape
    heads_here = width // HEAD_DIM
    ends = jnp.cumsum(lengths)
    places = lax.axis_index("ctx") * rows + jnp.arange(rows, dtype=jnp.int32)
    piece = lax.all_gather(jnp.stack([keys, values]), "ctx", axis=1, tiled=True)
    count = piece.shape[1]
    key_places = jnp.arange(count, dtype=jnp.int32)
    allowed = (key_places[None, :] <= places[:, None]) & (
        doc_of(key_places, ends)[None, :] == doc_of(places, ends)[:, None]
    )
    scores = jnp.einsum(
        "qhd,khd->hqk",
        queries.reshape(rows, heads_here, HEAD_DIM),
        piece[0].reshape(count, heads_here, HEAD_DIM),
        preferred_element_type=jnp.float32,
    )
    masked = jnp.where(allowed[None], scores * (1.0 / math.sqrt(HEAD_DIM)), NEG)
    weight = jnp.exp(masked - jnp.max(masked, axis=2, keepdims=True))
    total = jnp.sum(weight, axis=2)
    summed = jnp.einsum(
        "hqk,khd->hqd",
        weight.astype(jnp.bfloat16),
        piece[1].reshape(count, heads_here, HEAD_DIM),
        preferred_element_type=jnp.float32,
    )
    return (summed / total[..., None]).transpose(1, 0, 2).reshape(rows, width).astype(jnp.bfloat16)


def send(value, pairs):
    return lax.ppermute(value, "ctx", pairs)


def shift(value, steps):
    count = lax.axis_size("ctx")
    return send(value, [(i, i + steps) for i in range(count) if 0 <= i + steps < count])


def in_pairs(ctx, width):
    count = width // HEAD_DIM
    return ctx == 4 and count % 2 == 0 and count // 2 <= SLOT


def shards(streams, short_filter, decay_rate, residue, skip_gain, lengths, queries, keys):
    f32, bf16 = jnp.float32, jnp.bfloat16
    shape = jax.ShapeDtypeStruct
    rows, width = streams.shape[1:]
    half = width // 2
    modes = decay_rate.shape[1]
    tiles = width // LANES
    ctx = lax.axis_size("ctx")
    paired = in_pairs(ctx, width)
    halves = shape((rows, half), bf16)

    if paired:
        rim, q_near, q_far, k_near, k_far = call(
            pack, (shape((3, SHORT - 1, width), bf16), halves, halves, halves, halves), 3, 0,
            scratch=[pltpu.VMEM((3, 16, width), bf16), pltpu.SemaphoreType.DMA((5,))],
            space=HBM,
        )(*(pltpu.with_memory_space_constraint(a, pltpu.HBM) for a in (streams, queries, keys)))
        rim = shift(rim, 1)
        q1 = shift(q_near, -1)
        q2 = send(q_far, [(3, 1)])
        k1 = shift(k_near, 1)
        k2 = send(k_far, [(0, 2)])
    else:
        rim = shift(streams[:, rows - SHORT + 1 :, :], 1)

    states = (modes * tiles, LANES)
    gate, long, state, step, block, low, high = call(
        hyena_local,
        (
            shape((rows, width), f32),
            shape((rows * tiles, LANES), f32),
            shape(states, bf16),
            shape(states, f32),
            shape(states, f32),
            halves,
            halves,
        ),
        7,
        scratch=[
            pltpu.VMEM((rows * tiles, LANES), f32),
            pltpu.VMEM(states, f32),
            pltpu.VMEM(states, f32),
        ],
    )(lengths, streams, rim, short_filter, decay_rate.T, residue.T, skip_gain.reshape(tiles, LANES))

    if paired:
        va = send(high, [(0, 1)])
        v2 = send(low, [(0, 2)])
        hops = tuple(range(ctx - 1))
        parts = [shift(state, hop + 1) for hop in hops]
    else:
        every = lax.all_gather(state, "ctx").astype(f32)
        ends = jnp.cumsum(lengths)
        before = lax.axis_index("ctx") * rows - 1
        lasts = (jnp.arange(ctx, dtype=jnp.int32) + 1) * rows - 1
        same = (lasts <= before) & (
            doc_of(lasts, ends) == doc_of(jnp.reshape(before, (1,)), ends)
        )
        factor = jnp.where(same, (before - lasts) // rows, 0).astype(f32)
        weight = same.astype(f32)[:, None, None] * block[None] ** factor[:, None, None]
        parts = [jnp.sum(weight * every, axis=0)]
        hops = (0,)

    value, *split = call(
        functools.partial(hyena_cross, hops),
        (shape((rows, width), bf16),) + ((halves, halves) if paired else ()),
        5 + len(hops),
        scratch=[pltpu.VMEM((rows * tiles, LANES), f32)],
    )(lengths, step, block, long, gate, *parts)

    if not paired:
        return value, gathered_attention(lengths, queries, keys, value)

    near, other = split
    vb = send(near, [(1, 2), (2, 3)])
    wide = shape((rows, half + LANES), bf16)
    o_far = call(hub_far, wide, 6)(lengths, q2, keys, other, k1, va)
    far = send(o_far, [(1, 3)])
    means = (shape((rows, width), f32), shape((rows, 2 * LANES), f32))
    early = call(own_early, means, 5)(lengths, queries, keys, near, other)
    o_near = call(hub_near, wide, 9)(
        lengths, q1, keys, other, k1, va, vb, k2, v2
    )
    last = shift(o_near, 1)
    late = call(own_late, means, 10)(lengths, queries, keys, near, other, k1, va, vb, k2, v2)
    attended = call(merge, shape((rows, width), bf16), 6, 0)(
        *early, *late, last, far
    )
    return value, attended


def solution(mesh):
    placed = (
        P(None, ("groups", "ctx"), "tp"),
        P(None, None, "tp"),
        P("tp", None),
        P("tp", None),
        P("tp"),
        P("groups"),
        P(("groups", "ctx"), "tp"),
        P(("groups", "ctx"), "tp"),
    )

    return jax.shard_map(
        shards,
        mesh=mesh,
        in_specs=placed,
        out_specs=(P(("groups", "ctx"), "tp"), P(("groups", "ctx"), "tp")),
        check_vma=False,
    )
```

profile of v0, /device:TPU:0, one launch (start us, length us, event | category | flops | bytes accessed | tf_op | source)
XLA Modules:
  0.0 67.0 jit_solution(12875736889357860891)
XLA Ops:
  0.7 1.5 %shard_map.95 = (bf16[3,2,2048]{2,1,0:T(2,128)(2,1)S(1)}, bf16[128,1024]{1,0:T(8,128)(2,1)S(1)}, bf16[128,1024]{1,0:T(8,128)(2,1)S(1)}, bf16[128,1024]{1,0:T(8,128)(2,1)S(1)}, bf16[128,1024]{1,0:T(8,128)(2,1)S(1)}) custom-call(bf16[3,128,2048]{2,1,0:T(8,128)(2,1)} %streams_ref.3, bf16[128,2048]{1,0:T(8,128)(2,1)} %query_ref.3, bf16[128,2048]{1,0:T(8,128)(2,1)} %key_ref.7), custom_call_target="tpu_custom_call" | custom-call | flops 10000000 | bytes 4000000 | tf_op jit(solution)/shard_map/pallas_call | solution.py:504
  2.2 5.0 %collective-permute-start.4 = (bf16[128,1024]{1,0:T(8,128)(2,1)S(1)}, bf16[128,1024]{1,0:T(8,128)(2,1)S(1)}, u32[]{:S(2)}, u32[]{:S(2)}) collective-permute-start(bf16[128,1024]{1,0:T(8,128)(2,1)S(1)} %get-tuple-element.32), channel_id=1, source_target_pairs={{0,4},{4,8},{8,12},{1,5},{5,9},{9,13},{2,6},{6,10},{10,14},{3,7},{... | collective-permute-start | bytes 786440 | tf_op jit(solution)/shard_map/ppermute | solution.py:479
  7.1 0.7 %collective-permute-start.11 = (bf16[128,1024]{1,0:T(8,128)(2,1)S(1)}, bf16[128,1024]{1,0:T(8,128)(2,1)S(1)}, u32[]{:S(2)}, u32[]{:S(2)}) collective-permute-start(bf16[128,1024]{1,0:T(8,128)(2,1)S(1)} %get-tuple-element.39), channel_id=1, source_target_pairs={{12,4},{13,5},{14,6},{15,7},{28,20},{29,21},{30,22},{31,23}} | collective-permute-start | bytes 786440 | tf_op jit(solution)/shard_map/ppermute | solution.py:479
  7.8 4.1 %collective-permute-start = (bf16[3,2,2048]{2,1,0:T(2,128)(2,1)S(1)}, bf16[3,2,2048]{2,1,0:T(2,128)(2,1)S(1)}, u32[]{:S(2)}, u32[]{:S(2)}) collective-permute-start(bf16[3,2,2048]{2,1,0:T(2,128)(2,1)S(1)} %get-tuple-element.21), channel_id=1, source_target_pairs={{0,4},{4,8},{8,12},{1,5},{5,9},{9,13},{2,6},{6,10},{10,14},{3,7},{... | collective-permute-start | bytes 73736 | tf_op jit(solution)/shard_map/ppermute | solution.py:479
  11.9 1.5 %collective-permute-done.rim_ref = bf16[3,2,2048]{2,1,0:T(2,128)(2,1)S(1)} collective-permute-done((bf16[3,2,2048]{2,1,0:T(2,128)(2,1)S(1)}, bf16[3,2,2048]{2,1,0:T(2,128)(2,1)S(1)}, u32[]{:S(2)}, u32[]{:S(2)}) %collective-permute-start) | collective-permute-done | bytes 24608 | tf_op jit(solution)/shard_map/ppermute | solution.py:479
  13.4 5.8 %shard_map.96 = (f32[128,2048]{1,0:T(8,128)S(1)}, f32[2048,128]{1,0:T(8,128)S(1)}, bf16[256,128]{1,0:T(8,128)(2,1)S(1)}, f32[256,128]{1,0:T(8,128)S(1)}, f32[256...) custom-call(s32[2]{0:T(128)S(1)} %copy-done.6, bf16[3,128,2048]{2,1,0:T(8,128)(2,1)S(1)} %copy-done.1, ...), custom_call_target="tpu_custom_call" | custom-call | flops 10000000 | bytes 4000000 | tf_op jit(solution)/shard_map/pallas_call | solution.py:518
  19.2 0.0 copy-start
  19.3 6.9 %collective-permute-start.3 = (bf16[256,128]{1,0:T(8,128)(2,1)S(1)}, bf16[256,128]{1,0:T(8,128)(2,1)S(1)}, u32[]{:S(2)}, u32[]{:S(2)}) collective-permute-start(bf16[256,128]{1,0:T(8,128)(2,1)S(1)} %get-tuple-element.26), channel_id=1, source_target_pairs={{0,12},{1,13},{2,14},{3,15},{16,28},{17,29},{18,30},{19,31}} | collective-permute-start | bytes 196616 | tf_op jit(solution)/shard_map/ppermute | solution.py:479
  26.2 1.3 %collective-permute-start.2 = (bf16[256,128]{1,0:T(8,128)(2,1)S(1)}, bf16[256,128]{1,0:T(8,128)(2,1)S(1)}, u32[]{:S(2)}, u32[]{:S(2)}) collective-permute-start(bf16[256,128]{1,0:T(8,128)(2,1)S(1)} %get-tuple-element.26), channel_id=1, source_target_pairs={{0,8},{4,12},{1,9},{5,13},{2,10},{6,14},{3,11},{7,15},{16,24},{20,... | collective-permute-start | bytes 196616 | tf_op jit(solution)/shard_map/ppermute | solution.py:479
  27.5 2.5 %collective-permute-start.1 = (bf16[256,128]{1,0:T(8,128)(2,1)S(1)}, bf16[256,128]{1,0:T(8,128)(2,1)S(1)}, u32[]{:S(2)}, u32[]{:S(2)}) collective-permute-start(bf16[256,128]{1,0:T(8,128)(2,1)S(1)} %get-tuple-element.26), channel_id=1, source_target_pairs={{0,4},{4,8},{8,12},{1,5},{5,9},{9,13},{2,6},{6,10},{10,14},{3,7},{... | collective-permute-start | bytes 196616 | tf_op jit(solution)/shard_map/ppermute | solution.py:479
  30.0 1.3 %collective-permute-start.7 = (bf16[128,1024]{1,0:T(8,128)(2,1)S(1)}, bf16[128,1024]{1,0:T(8,128)(2,1)S(1)}, u32[]{:S(2)}, u32[]{:S(2)}) collective-permute-start(bf16[128,1024]{1,0:T(8,128)(2,1)S(1)} %get-tuple-element.34), channel_id=1, source_target_pairs={{0,8},{1,9},{2,10},{3,11},{16,24},{17,25},{18,26},{19,27}} | collective-permute-start | bytes 786440 | tf_op jit(solution)/shard_map/ppermute | solution.py:479
  31.3 1.3 %collective-permute-start.9 = (bf16[128,1024]{1,0:T(8,128)(2,1)S(1)}, bf16[128,1024]{1,0:T(8,128)(2,1)S(1)}, u32[]{:S(2)}, u32[]{:S(2)}) collective-permute-start(bf16[128,1024]{1,0:T(8,128)(2,1)S(1)} %get-tuple-element.38), channel_id=1, source_target_pairs={{4,0},{8,4},{12,8},{5,1},{9,5},{13,9},{6,2},{10,6},{14,10},{7,3},{... | collective-permute-start | bytes 786440 | tf_op jit(solution)/shard_map/ppermute | solution.py:479
  32.6 4.6 %collective-permute-start.5 = (bf16[128,1024]{1,0:T(8,128)(2,1)S(1)}, bf16[128,1024]{1,0:T(8,128)(2,1)S(1)}, u32[]{:S(2)}, u32[]{:S(2)}) collective-permute-start(bf16[128,1024]{1,0:T(8,128)(2,1)S(1)} %get-tuple-element.33), channel_id=1, source_target_pairs={{0,4},{1,5},{2,6},{3,7},{16,20},{17,21},{18,22},{19,23}} | collective-permute-start | bytes 786440 | tf_op jit(solution)/shard_map/ppermute | solution.py:479
  37.2 2.5 %shard_map.97 = (bf16[128,2048]{1,0:T(8,128)(2,1)}, bf16[128,1024]{1,0:T(8,128)(2,1)S(1)}, bf16[128,1024]{1,0:T(8,128)(2,1)S(1)}) custom-call(s32[2]{0:T(128)S(1)} %copy-done.6, f32[256,128]{1,0:T(8,128)S(1)} %get-tuple-element.22.step_ref, f32[256,128]{1,0:T(8,128)S(1)} %get-tuple-element.23.block_ref, f32[2048,128]{1,0:T(8,128)S(1)} %get-tuple-element.24.long_ref, ...), custom_call_target="tpu_custom_call" | custom-call | flops 10000000 | bytes 4000000 | tf_op jit(solution)/shard_map/pallas_call | solution.py:555
  39.7 5.1 %collective-permute-start.8 = (bf16[128,1024]{1,0:T(8,128)(2,1)S(1)}, bf16[128,1024]{1,0:T(8,128)(2,1)S(1)}, u32[]{:S(2)}, u32[]{:S(2)}) collective-permute-start(bf16[128,1024]{1,0:T(8,128)(2,1)S(1)} %get-tuple-element.35), channel_id=1, source_target_pairs={{0,8},{1,9},{2,10},{3,11},{16,24},{17,25},{18,26},{19,27}} | collective-permute-start | bytes 786440 | tf_op jit(solution)/shard_map/ppermute | solution.py:479
  44.8 0.7 %collective-permute-start.6 = (bf16[128,1024]{1,0:T(8,128)(2,1)S(1)}, bf16[128,1024]{1,0:T(8,128)(2,1)S(1)}, u32[]{:S(2)}, u32[]{:S(2)}) collective-permute-start(bf16[128,1024]{1,0:T(8,128)(2,1)S(1)} %get-tuple-element.28.near_ref), channel_id=1, source_target_pairs={{4,8},{8,12},{5,9},{9,13},{6,10},{10,14},{7,11},{11,15},{20,24},{2... | collective-permute-start | bytes 786440 | tf_op jit(solution)/shard_map/ppermute | solution.py:479
  45.5 0.6 shard_map.101
  46.0 0.8 %collective-permute-start.12 = (bf16[128,1152]{1,0:T(8,128)(2,1)S(1)}, bf16[128,1152]{1,0:T(8,128)(2,1)S(1)}, u32[]{:S(2)}, u32[]{:S(2)}) collective-permute-start(bf16[128,1152]{1,0:T(8,128)(2,1)S(1)} %shard_map.101), channel_id=1, source_target_pairs={{4,12},{5,13},{6,14},{7,15},{20,28},{21,29},{22,30},{23,31}} | collective-permute-start | bytes 884744 | tf_op jit(solution)/shard_map/ppermute | solution.py:479
  46.9 1.8 %collective-permute-done.8.v2_ref = bf16[128,1024]{1,0:T(8,128)(2,1)S(1)} collective-permute-done((bf16[128,1024]{1,0:T(8,128)(2,1)S(1)}, bf16[128,1024]{1,0:T(8,128)(2,1)S(1)}, u32[]{:S(2)}, u32[]{:S(2)}) %collective-permute-start.8) | collective-permute-done | bytes 262176 | tf_op jit(solution)/shard_map/ppermute | solution.py:479
  48.7 2.7 %shard_map.100 = bf16[128,1152]{1,0:T(8,128)(2,1)S(1)} custom-call(s32[2]{0:T(128)S(1)} %copy-done.6, bf16[128,1024]{1,0:T(8,128)(2,1)S(1)} %collective-permute-done.9.q1_ref, bf16[128,2048]{1,0:T(8,128)(2,1)S(1)} %copy-done, bf16[128,1024]{1,0:T(8,128)(2,1)S(1)} %get-tuple-element.29.other_ref, bf16[128,1024]{1,0:T(8,128)(2,1)S(1)} %collective-permute-done.4.k1_ref, ...), custom_call_target="tpu_custom_call" | custom-call | flops 10000000 | bytes 4000000 | tf_op jit(solution)/shard_map/pallas_call | solution.py:572
  51.4 9.3 %collective-permute-start.10 = (bf16[128,1152]{1,0:T(8,128)(2,1)S(1)}, bf16[128,1152]{1,0:T(8,128)(2,1)S(1)}, u32[]{:S(2)}, u32[]{:S(2)}) collective-permute-start(bf16[128,1152]{1,0:T(8,128)(2,1)S(1)} %shard_map.100), channel_id=1, source_target_pairs={{0,4},{4,8},{8,12},{1,5},{5,9},{9,13},{2,6},{6,10},{10,14},{3,7},{... | collective-permute-start | bytes 884744 | tf_op jit(solution)/shard_map/ppermute | solution.py:479
  60.7 4.8 %shard_map.98 = (f32[128,2048]{1,0:T(8,128)S(1)}, f32[128,256]{1,0:T(8,128)S(1)}) custom-call(s32[2]{0:T(128)S(1)} %copy-done.6, bf16[128,2048]{1,0:T(8,128)(2,1)S(1)} %copy-done.2, bf16[128,2048]{1,0:T(8,128)(2,1)S(1)} %copy-done, bf16[128,1024]{1,0:T(8,128)(2,1)S(1)} %get-tuple-element.28.near_ref, bf16[128,1024]{1,0:T(8,128)(2,1)S(1)} %get-tuple-element.29.other_ref), custom_call_target="tpu_custom_call" | custom-call | flops 10000000 | bytes 4000000 | tf_op jit(solution)/shard_map/pallas_call | solution.py:571
  65.5 0.6 shard_map.99
  66.1 0.9 %shard_map.102 = bf16[128,2048]{1,0:T(8,128)(2,1)} custom-call(f32[128,2048]{1,0:T(8,128)S(1)} %get-tuple-element.30.early_ref, f32[128,256]{1,0:T(8,128)S(1)} %get-tuple-element.31.early_stat, f32[128,2048]{1,0:T(8,128)S(1)} %get-tuple-element.36.late_ref, f32[128,256]{1,0:T(8,128)S(1)} %get-tuple-element.37.late_stat, ...), custom_call_target="tpu_custom_call" | custom-call | flops 10000000 | bytes 4000000 | tf_op jit(solution)/shard_map/pallas_call | solution.py:577
  (26 shorter events, 0.1 us)
Async XLA Ops:
  0.6 12.8 %copy-start.1 = (bf16[3,128,2048]{2,1,0:T(8,128)(2,1)S(1)}, bf16[3,128,2048]{2,1,0:T(8,128)(2,1)}, u32[]{:S(2)}) copy-start(bf16[3,128,2048]{2,1,0:T(8,128)(2,1)} %streams_ref.3) | copy-start | bytes 4718596
  0.6 12.8 %copy-start.6 = (s32[2]{0:T(128)S(1)}, s32[2]{0:T(128)}, u32[]{:S(2)}) copy-start(s32[2]{0:T(128)} %lengths_ref.11) | copy-start | bytes 28
  0.7 12.8 %copy-start.7 = (f32[2048]{0:T(1024)S(1)}, f32[2048]{0:T(1024)}, u32[]{:S(2)}) copy-start(f32[2048]{0:T(1024)} %param.12) | copy-start | bytes 24580
  0.7 12.8 %copy-start.4 = (f32[2048,16]{0,1:T(8,128)S(1)}, f32[2048,16]{0,1:T(8,128)}, u32[]{:S(2)}) copy-start(f32[2048,16]{0,1:T(8,128)} %param.11) | copy-start | bytes 393220
  0.7 12.8 %copy-start.3 = (f32[2048,16]{0,1:T(8,128)S(1)}, f32[2048,16]{0,1:T(8,128)}, u32[]{:S(2)}) copy-start(f32[2048,16]{0,1:T(8,128)} %param.10) | copy-start | bytes 393220
  0.7 12.8 %copy-start.5 = (f32[3,3,2048]{2,1,0:T(4,128)S(1)}, f32[3,3,2048]{2,1,0:T(4,128)}, u32[]{:S(2)}) copy-start(f32[3,3,2048]{2,1,0:T(4,128)} %taps_ref.1) | copy-start | bytes 221188
  2.2 37.5 %collective-permute-start.4 = (bf16[128,1024]{1,0:T(8,128)(2,1)S(1)}, bf16[128,1024]{1,0:T(8,128)(2,1)S(1)}, u32[]{:S(2)}, u32[]{:S(2)}) collective-permute-start(bf16[128,1024]{1,0:T(8,128)(2,1)S(1)} %get-tuple-element.32), channel_id=1, source_target_pairs={{0,4},{4,8},{8,12},{1,5},{5,9},{9,13},{2,6},{6,10},{10,14},{3,7},{... | collective-permute-start | bytes 786440 | tf_op jit(solution)/shard_map/ppermute | solution.py:479
  7.1 37.6 %collective-permute-start.11 = (bf16[128,1024]{1,0:T(8,128)(2,1)S(1)}, bf16[128,1024]{1,0:T(8,128)(2,1)S(1)}, u32[]{:S(2)}, u32[]{:S(2)}) collective-permute-start(bf16[128,1024]{1,0:T(8,128)(2,1)S(1)} %get-tuple-element.39), channel_id=1, source_target_pairs={{12,4},{13,5},{14,6},{15,7},{28,20},{29,21},{30,22},{31,23}} | collective-permute-start | bytes 786440 | tf_op jit(solution)/shard_map/ppermute | solution.py:479
  7.8 5.6 %collective-permute-start = (bf16[3,2,2048]{2,1,0:T(2,128)(2,1)S(1)}, bf16[3,2,2048]{2,1,0:T(2,128)(2,1)S(1)}, u32[]{:S(2)}, u32[]{:S(2)}) collective-permute-start(bf16[3,2,2048]{2,1,0:T(2,128)(2,1)S(1)} %get-tuple-element.21), channel_id=1, source_target_pairs={{0,4},{4,8},{8,12},{1,5},{5,9},{9,13},{2,6},{6,10},{10,14},{3,7},{... | collective-permute-start | bytes 73736 | tf_op jit(solution)/shard_map/ppermute | solution.py:479
  19.2 26.2 %copy-start = (bf16[128,2048]{1,0:T(8,128)(2,1)S(1)}, bf16[128,2048]{1,0:T(8,128)(2,1)}, u32[]{:S(2)}) copy-start(bf16[128,2048]{1,0:T(8,128)(2,1)} %key_ref.7) | copy-start | bytes 1572868
  19.3 10.7 %collective-permute-start.3 = (bf16[256,128]{1,0:T(8,128)(2,1)S(1)}, bf16[256,128]{1,0:T(8,128)(2,1)S(1)}, u32[]{:S(2)}, u32[]{:S(2)}) collective-permute-start(bf16[256,128]{1,0:T(8,128)(2,1)S(1)} %get-tuple-element.26), channel_id=1, source_target_pairs={{0,12},{1,13},{2,14},{3,15},{16,28},{17,29},{18,30},{19,31}} | collective-permute-start | bytes 196616 | tf_op jit(solution)/shard_map/ppermute | solution.py:479
  26.2 5.1 %collective-permute-start.2 = (bf16[256,128]{1,0:T(8,128)(2,1)S(1)}, bf16[256,128]{1,0:T(8,128)(2,1)S(1)}, u32[]{:S(2)}, u32[]{:S(2)}) collective-permute-start(bf16[256,128]{1,0:T(8,128)(2,1)S(1)} %get-tuple-element.26), channel_id=1, source_target_pairs={{0,8},{4,12},{1,9},{5,13},{2,10},{6,14},{3,11},{7,15},{16,24},{20,... | collective-permute-start | bytes 196616 | tf_op jit(solution)/shard_map/ppermute | solution.py:479
  27.5 5.1 %collective-permute-start.1 = (bf16[256,128]{1,0:T(8,128)(2,1)S(1)}, bf16[256,128]{1,0:T(8,128)(2,1)S(1)}, u32[]{:S(2)}, u32[]{:S(2)}) collective-permute-start(bf16[256,128]{1,0:T(8,128)(2,1)S(1)} %get-tuple-element.26), channel_id=1, source_target_pairs={{0,4},{4,8},{8,12},{1,5},{5,9},{9,13},{2,6},{6,10},{10,14},{3,7},{... | collective-permute-start | bytes 196616 | tf_op jit(solution)/shard_map/ppermute | solution.py:479
  30.0 16.9 %collective-permute-start.7 = (bf16[128,1024]{1,0:T(8,128)(2,1)S(1)}, bf16[128,1024]{1,0:T(8,128)(2,1)S(1)}, u32[]{:S(2)}, u32[]{:S(2)}) collective-permute-start(bf16[128,1024]{1,0:T(8,128)(2,1)S(1)} %get-tuple-element.34), channel_id=1, source_target_pairs={{0,8},{1,9},{2,10},{3,11},{16,24},{17,25},{18,26},{19,27}} | collective-permute-start | bytes 786440 | tf_op jit(solution)/shard_map/ppermute | solution.py:479
  31.3 15.6 %collective-permute-start.9 = (bf16[128,1024]{1,0:T(8,128)(2,1)S(1)}, bf16[128,1024]{1,0:T(8,128)(2,1)S(1)}, u32[]{:S(2)}, u32[]{:S(2)}) collective-permute-start(bf16[128,1024]{1,0:T(8,128)(2,1)S(1)} %get-tuple-element.38), channel_id=1, source_target_pairs={{4,0},{8,4},{12,8},{5,1},{9,5},{13,9},{6,2},{10,6},{14,10},{7,3},{... | collective-permute-start | bytes 786440 | tf_op jit(solution)/shard_map/ppermute | solution.py:479
  32.6 12.8 %collective-permute-start.5 = (bf16[128,1024]{1,0:T(8,128)(2,1)S(1)}, bf16[128,1024]{1,0:T(8,128)(2,1)S(1)}, u32[]{:S(2)}, u32[]{:S(2)}) collective-permute-start(bf16[128,1024]{1,0:T(8,128)(2,1)S(1)} %get-tuple-element.33), channel_id=1, source_target_pairs={{0,4},{1,5},{2,6},{3,7},{16,20},{17,21},{18,22},{19,23}} | collective-permute-start | bytes 786440 | tf_op jit(solution)/shard_map/ppermute | solution.py:479
  39.7 9.0 %collective-permute-start.8 = (bf16[128,1024]{1,0:T(8,128)(2,1)S(1)}, bf16[128,1024]{1,0:T(8,128)(2,1)S(1)}, u32[]{:S(2)}, u32[]{:S(2)}) collective-permute-start(bf16[128,1024]{1,0:T(8,128)(2,1)S(1)} %get-tuple-element.35), channel_id=1, source_target_pairs={{0,8},{1,9},{2,10},{3,11},{16,24},{17,25},{18,26},{19,27}} | collective-permute-start | bytes 786440 | tf_op jit(solution)/shard_map/ppermute | solution.py:479
  44.8 3.9 %collective-permute-start.6 = (bf16[128,1024]{1,0:T(8,128)(2,1)S(1)}, bf16[128,1024]{1,0:T(8,128)(2,1)S(1)}, u32[]{:S(2)}, u32[]{:S(2)}) collective-permute-start(bf16[128,1024]{1,0:T(8,128)(2,1)S(1)} %get-tuple-element.28.near_ref), channel_id=1, source_target_pairs={{4,8},{8,12},{5,9},{9,13},{6,10},{10,14},{7,11},{11,15},{20,24},{2... | collective-permute-start | bytes 786440 | tf_op jit(solution)/shard_map/ppermute | solution.py:479
  46.0 14.6 %copy-start.2 = (bf16[128,2048]{1,0:T(8,128)(2,1)S(1)}, bf16[128,2048]{1,0:T(8,128)(2,1)}, u32[]{:S(2)}) copy-start(bf16[128,2048]{1,0:T(8,128)(2,1)} %query_ref.3) | copy-start | bytes 1572868
  46.0 20.0 %collective-permute-start.12 = (bf16[128,1152]{1,0:T(8,128)(2,1)S(1)}, bf16[128,1152]{1,0:T(8,128)(2,1)S(1)}, u32[]{:S(2)}, u32[]{:S(2)}) collective-permute-start(bf16[128,1152]{1,0:T(8,128)(2,1)S(1)} %shard_map.101), channel_id=1, source_target_pairs={{4,12},{5,13},{6,14},{7,15},{20,28},{21,29},{22,30},{23,31}} | collective-permute-start | bytes 884744 | tf_op jit(solution)/shard_map/ppermute | solution.py:479
  51.4 14.7 %collective-permute-start.10 = (bf16[128,1152]{1,0:T(8,128)(2,1)S(1)}, bf16[128,1152]{1,0:T(8,128)(2,1)S(1)}, u32[]{:S(2)}, u32[]{:S(2)}) collective-permute-start(bf16[128,1152]{1,0:T(8,128)(2,1)S(1)} %shard_map.100), channel_id=1, source_target_pairs={{0,4},{4,8},{8,12},{1,5},{5,9},{9,13},{2,6},{6,10},{10,14},{3,7},{... | collective-permute-start | bytes 884744 | tf_op jit(solution)/shard_map/ppermute | solution.py:479
where the time goes:
time: 67.4 us; the launch traced here: 67 us
  starting transfers between devices  43.4 us (64%)
  Pallas kernels  19.2 us (28%)
  waiting for transfers between devices  3.3 us (5%)
  between operations  0.95 us (1%)
    ppermute x13, starting transfers between devices, send(): return lax.ppermute(value, 'ctx', pairs)  43.4 us
    pallas_call x1, Pallas kernels, shards(): call(hyena_local, (shape((rows, width), f32), shape((rows * tiles, LANES)...  5.79 us
    pallas_call x1, Pallas kernels, shards(): early = call(own_early, means, 5)(lengths, queries, keys, near, other)  4.82 us
    ppermute x13, waiting for transfers between devices, send(): return lax.ppermute(value, 'ctx', pairs)  3.3 us
    pallas_call x1, Pallas kernels, shards(): call(hub_near, wide, 9)(lengths, q1, keys, other, k1, va, vb, k2, v2)  2.71 us
    pallas_call x1, Pallas kernels, shards(): call(functools.partial(hyena_cross, hops), (shape((rows, width), bf16),)...  2.45 us
    pallas_call x1, Pallas kernels, shards(): call(pack, (shape((3, SHORT - 1, width), bf16), halves, halves, halves, h...  1.46 us
  transfers between devices with their start and end apart: 13, of which 2 were waited for; matrix products, arithmetic and copies ran while one was open for 0% of the time, Pallas kernels for 25%

commit v1 on v0

--- a/solution.py
+++ b/solution.py
@@ -56,12 +56,11 @@
 
 
 def hyena_local(lengths_ref, streams_ref, rim_ref, taps_ref, decay_ref, residue_ref, skip_ref,
-                gate_ref, long_ref, state_ref, step_ref, block_ref, low_ref, high_ref,
+                gate_ref, long_ref, state_ref, step_ref, block_ref,
                 mixed_ref, gain_ref, final_ref):
     rows, width = gate_ref.shape
     modes = decay_ref.shape[0]
     tiles = width // LANES
-    half = width // 2
     index = lax.axis_index("ctx")
     first = index * rows
     ends = ends_of(lengths_ref)
@@ -131,18 +130,10 @@
             low = high
     state_ref[...] = final_ref[...].astype(state_ref.dtype)
 
-    @pl.when(index == 0)
-    def _():
-        for j in range(tiles):
-            lanes = slice(j * LANES, (j + 1) * LANES)
-            value = gate_ref[:, lanes] * long_ref[pl.ds(j, rows, stride=tiles), :]
-            out, at = (low_ref, j) if j * LANES < half else (high_ref, j - tiles // 2)
-            out[:, at * LANES : (at + 1) * LANES] = value.astype(out.dtype)
-
 
 def hyena_cross(hops, lengths_ref, step_ref, block_ref, long_ref, gate_ref, *refs):
     parts = refs[: len(hops)]
-    value_ref, *halves, cross_ref = refs[len(hops) :]
+    value_ref, cross_ref = refs[len(hops) :]
     rows, width = gate_ref.shape
     tiles = width // LANES
     modes = step_ref.shape[0] // tiles
@@ -199,46 +190,140 @@
         long = long_ref[every, :] + jnp.where(reached, cross_ref[every, :], 0.0)
         value_ref[:, lanes] = (gate_ref[:, lanes] * long).astype(value_ref.dtype)
 
-    if halves:
-        near_ref, other_ref = halves
-        odd = index % 2 == 1
-        copy_half(value_ref, near_ref, odd)
-        copy_half(value_ref, other_ref, jnp.logical_not(odd))
-
-
-def copy_half(source_ref, target_ref, lower):
-    half = target_ref.shape[1]
-
-    @pl.when(lower)
-    def _():
-        target_ref[...] = source_ref[:, :half]
-
-    @pl.when(jnp.logical_not(lower))
-    def _():
-        target_ref[...] = source_ref[:, half:]
-
-
-def pack(streams_ref, queries_ref, keys_ref, rim_ref, q_near, q_far, k_near, k_far, tail_ref, sems):
+
+def tree_sum(terms):
+    while len(terms) > 1:
+        odd = [terms[-1]] if len(terms) % 2 else []
+        terms = [a + b for a, b in zip(terms[::2], terms[1::2])] + odd
+    return terms[0]
+
+
+def stage(me, last, lengths_ref, streams_ref, taps_ref, decay_ref, residue_ref, skip_ref, *refs):
+    refs = list(refs)
+    carry_ref = refs.pop(0) if me else None
+    near_ref, other_ref = refs[:2]
+    next_ref = None if last else refs[2]
+    gate_ref, mixed_ref, long_ref, step_ref, gain_ref, carried_ref, shifted_ref = refs[-7:]
+    rows, half = near_ref.shape
+    width = 2 * half
+    modes = decay_ref.shape[0]
+    tiles = width // LANES
+    states = modes * tiles
+    first = me * rows
     reach_back = SHORT - 1
-    rows, half = q_far.shape
-    tail = tail_ref.shape[1]
+
+    def run():
+        ends = ends_of(lengths_ref)
+        start = start_of(jnp.int32(first), ends)
+        goes_on = [(start <= first - i).astype(jnp.float32) for i in range(1, SHORT)]
+        if me:
+            carried_ref[...] = carry_ref[...].astype(jnp.float32)
+        edges = {}
+        if me:
+            for s in range(3):
+                for k in range(1, SHORT):
+                    at = states + (s * reach_back + reach_back - k) * tiles
+                    edges[s, k] = carried_ref[at : at + tiles, :] * goes_on[k - 1]
+        for j in range(tiles):
+            lanes = slice(j * LANES, (j + 1) * LANES)
+            filtered = []
+            for s in range(3):
+                x = streams_ref[s, :, lanes].astype(jnp.float32)
+                total = taps_ref[0, s : s + 1, lanes] * x
+                for i in range(1, SHORT):
+                    buffer = shifted_ref.at[j % 2, s, i - 1]
+                    buffer[8 : 8 + rows, :] = x
+                    for k in range(1, i + 1):
+                        edge = edges[s, k][j : j + 1, :] if me else jnp.zeros((1, LANES), jnp.float32)
+                        buffer[8 - k : 9 - k, :] = edge
+                    for end in ends[:-1]:
+                        inside = (end > first) & (end < first + rows)
+                        for k in range(1, i + 1):
+                            at = jnp.where(inside, 8 + end - first - k, rows + 8)
+                            buffer[pl.ds(at, 1), :] = jnp.zeros((1, LANES), jnp.float32)
+                    total = total + taps_ref[i, s : s + 1, lanes] * buffer[8 - i : 8 - i + rows, :]
+                filtered.append(total)
+                if not last:
+                    for k in range(reach_back):
+                        at = states + (s * reach_back + k) * tiles + j
+                        row = rows - reach_back + k
+                        carried_ref[at : at + 1, :] = x[row : row + 1, :]
+            gate_ref[:, lanes] = filtered[0]
+            mixed_ref[pl.ds(j, rows, stride=tiles), :] = filtered[1] * filtered[2]
+            step_ref[pl.ds(j, modes, stride=tiles), :] = jnp.exp(-decay_ref[:, lanes])
+            gain_ref[pl.ds(j, modes, stride=tiles), :] = residue_ref[:, lanes]
+
+        for h in range(tiles // 8):
+            spots = [slice(m * tiles + h * 8, m * tiles + h * 8 + 8) for m in range(modes)]
+            decay = [step_ref[at, :] for at in spots]
+            gain = [gain_ref[at, :] for at in spots]
+            skip = skip_ref[h * 8 : h * 8 + 8, :]
+
+            def advance(t, state):
+                at = pl.ds(pl.multiple_of(t * tiles + h * 8, 8), 8)
+                x = mixed_ref[at, :]
+                state = tuple(s * d + g * x for s, d, g in zip(state, decay, gain))
+                long_ref[at, :] = tree_sum(list(state) + [skip * x])
+                return state
+
+            incoming = [carried_ref[at, :] * goes_on[0] for at in spots] if me else None
+            low = jnp.int32(0)
+            for end in ends:
+                high = jnp.clip(end - first, 0, rows)
+
+                def four(g, state, low=low):
+                    for u in range(4):
+                        state = advance(low + g * 4 + u, state)
+                    return state
+
+                groups = lax.shift_right_logical(high - low, 2)
+                if me:
+                    at_start = (low == 0).astype(jnp.float32)
+                    state = tuple(s * at_start for s in incoming)
+                else:
+                    state = tuple(jnp.zeros((8, LANES), jnp.float32) for _ in spots)
+                state = lax.fori_loop(0, groups, four, state)
+                state = lax.fori_loop(low + groups * 4, high, advance, state)
+                if not last:
+
+                    @pl.when((low < high) & (high == rows))
+                    def _(state=state):
+                        for at, s in zip(spots, state):
+                            carried_ref[at, :] = s
+
+                low = high
+        if not last:
+            next_ref[...] = carried_ref[...].astype(next_ref.dtype)
+        lower, upper = (near_ref, other_ref) if me % 2 else (other_ref, near_ref)
+        for j in range(tiles):
+            long = long_ref[pl.ds(j, rows, stride=tiles), :]
+            value = gate_ref[:, j * LANES : (j + 1) * LANES] * long
+            out, at = (lower, j) if j < tiles // 2 else (upper, j - tiles // 2)
+            out[:, at * LANES : (at + 1) * LANES] = value.astype(out.dtype)
+
+    pl.when(lax.axis_index("ctx") == me)(run)
+
+
+def pack(queries_ref, keys_ref, *refs):
+    count = (len(refs) - 5) // 2
+    given, (q_near, q_far, k_near, k_far), held = refs[:count], refs[count:][:4], refs[count + 4 : -1]
+    sems = refs[-1]
+    half = q_far.shape[1]
     even = 1 - lax.axis_index("ctx") % 2
     near = pl.ds(pl.multiple_of(even * half, half), half)
     copies = [
         pltpu.make_async_copy(source, target, sems.at[i])
         for i, (source, target) in enumerate((
-            (streams_ref.at[:, rows - tail :, :], tail_ref),
+            *zip(given, held),
+            (queries_ref.at[:, half:], q_far),
             (keys_ref.at[:, near], k_near),
             (keys_ref.at[:, :half], k_far),
             (queries_ref.at[:, near], q_near),
-            (queries_ref.at[:, half:], q_far),
         ))
     ]
     for copy in copies:
         copy.start()
-    copies[0].wait()
-    rim_ref[...] = tail_ref[:, tail - reach_back :, :]
-    for copy in copies[1:]:
+    for copy in copies:
         copy.wait()
 
 
@@ -252,27 +337,18 @@
     return out
 
 
-def one_head(query, pairs, bias):
+def one_head(query, keys, values, bias):
     scale = 1.0 / math.sqrt(HEAD_DIM)
     base2 = scale * math.log2(math.e)
-    dims = (((1,), (1,)), ((), ()))
-    scores = [
-        lax.dot_general(query, key, dims, preferred_element_type=jnp.float32) + b
-        for (key, _), b in zip(pairs, bias)
-    ]
-    top = scores[0]
-    for s in scores[1:]:
-        top = jnp.maximum(top, s)
-    top = jnp.max(top, axis=1, keepdims=True)
-    weights = [jnp.exp2((s - top) * base2) for s in scores]
-    total = weights[0]
-    for w in weights[1:]:
-        total = total + w
-    total = jnp.sum(total, axis=1, keepdims=True)
-    summed = None
-    for w, (_, value) in zip(weights, pairs):
-        part = jnp.dot(w.astype(jnp.bfloat16), value, preferred_element_type=jnp.float32)
-        summed = part if summed is None else summed + part
+    key = keys[0] if len(keys) == 1 else jnp.concatenate(keys, axis=0)
+    value = values[0] if len(values) == 1 else jnp.concatenate(values, axis=0)
+    scores = lax.dot_general(
+        query, key, (((1,), (1,)), ((), ())), preferred_element_type=jnp.float32
+    ) + bias
+    top = jnp.max(scores, axis=1, keepdims=True)
+    weights = jnp.exp2((scores - top) * base2)
+    total = jnp.sum(weights, axis=1, keepdims=True)
+    summed = jnp.dot(weights.astype(jnp.bfloat16), value, preferred_element_type=jnp.float32)
     return summed / total, top * scale + jnp.log(total)
 
 
@@ -289,10 +365,13 @@
 
 
 def attend(query_block, query_ref, query_at, sources, rows, count, ends, write):
-    bias = biases(query_block, [block for block, _, _, _ in sources], rows, ends)
+    bias = jnp.concatenate(
+        biases(query_block, [block for block, _, _, _ in sources], rows, ends), axis=1
+    )
     for h in range(count):
-        pairs = [(cut(keys, at + h), cut(values, h)) for _, keys, at, values in sources]
-        write(h, *one_head(cut(query_ref, query_at + h), pairs, bias))
+        held_keys = [cut(keys, at + h) for _, keys, at, _ in sources]
+        held_values = [cut(values, h) for _, _, _, values in sources]
+        write(h, *one_head(cut(query_ref, query_at + h), held_keys, held_values, bias))
 
 
 def serve(query_block, query_ref, sources, ends, out_ref):
@@ -318,25 +397,26 @@
         serve(3, q2_ref, sources, ends_of(lengths_ref), far_ref)
 
 
-def hub_near(lengths_ref, q1_ref, key_ref, other_ref, k1_ref, va_ref, vb_ref, k2_ref, v2_ref,
-             near_ref):
+def hub_mid(lengths_ref, q1_ref, key_ref, other0, other1, k1_ref, va_ref, near_ref):
     count = q1_ref.shape[1] // HEAD_DIM
     index = lax.axis_index("ctx")
     ends = ends_of(lengths_ref)
 
     @pl.when(index == 0)
     def _():
-        serve(1, q1_ref, [(0, key_ref, 0, other_ref)], ends, near_ref)
+        serve(1, q1_ref, [(0, key_ref, 0, other0)], ends, near_ref)
 
     @pl.when(index == 1)
     def _():
-        sources = [(1, key_ref, count, other_ref), (0, k1_ref, 0, va_ref)]
+        sources = [(1, key_ref, count, other1), (0, k1_ref, 0, va_ref)]
         serve(2, q1_ref, sources, ends, near_ref)
 
-    @pl.when(index == 2)
+
+def hub_last(lengths_ref, q1_ref, key_ref, other_ref, k1_ref, vb_ref, k2_ref, v2_ref, near_ref):
+    @pl.when(lax.axis_index("ctx") == 2)
     def _():
         sources = [(2, key_ref, 0, other_ref), (1, k1_ref, 0, vb_ref), (0, k2_ref, 0, v2_ref)]
-        serve(3, q1_ref, sources, ends, near_ref)
+        serve(3, q1_ref, sources, ends_of(lengths_ref), near_ref)
 
 
 def own_half(query_ref, key_ref, mean_ref, stat_ref, ends, base, values, more=()):
@@ -354,7 +434,8 @@
     stat_ref[:, (LANES if base else 0) : (2 * LANES if base else LANES)] = stats[0]
 
 
-def own_early(lengths_ref, query_ref, key_ref, near_ref, other_ref, mean_ref, stat_ref):
+def own_early(lengths_ref, query_ref, key_ref, k1_ref, va_ref, near0, near1, near2, other0, other1,
+              mean_ref, stat_ref):
     count = query_ref.shape[1] // HEAD_DIM // 2
     index = lax.axis_index("ctx")
     run = functools.partial(
@@ -363,40 +444,47 @@
 
     @pl.when(index == 0)
     def _():
-        run(0, other_ref)
-
-    @pl.when(index == 3)
-    def _():
-        run(0, near_ref)
-
-    @pl.when(index % 2 == 0)
-    def _():
-        run(count, near_ref)
-
-
-def own_late(lengths_ref, query_ref, key_ref, near_ref, other_ref, k1_ref, va_ref, vb_ref, k2_ref,
-             v2_ref, mean_ref, stat_ref):
+        run(0, other0)
+        run(count, near0)
+
+    @pl.when(index == 1)
+    def _():
+        run(0, near1)
+        run(count, other1, [(0, k1_ref, 0, va_ref)])
+
+    @pl.when(index == 2)
+    def _():
+        run(count, near2)
+
+
+def own_late(lengths_ref, query_ref, key_ref, k1_ref, vb_ref, vc_ref, k2_ref, v2_ref,
+             near0, near1, near2, near3, other0, other1, other2, other3,
+             value_ref, mean_ref, stat_ref):
     count = query_ref.shape[1] // HEAD_DIM // 2
+    half = near0.shape[1]
     index = lax.axis_index("ctx")
     run = functools.partial(
         own_half, query_ref, key_ref, mean_ref, stat_ref, ends_of(lengths_ref)
     )
-
-    @pl.when(index == 1)
-    def _():
-        run(0, near_ref)
-        run(count, other_ref, [(0, k1_ref, 0, va_ref)])
+    for me, (lower, upper) in enumerate(
+        ((other0, near0), (near1, other1), (other2, near2), (near3, other3))
+    ):
+        @pl.when(index == me)
+        def _(lower=lower, upper=upper):
+            value_ref[:, :half] = lower[...]
+            value_ref[:, half:] = upper[...]
 
     @pl.when(index == 2)
     def _():
-        run(0, other_ref, [(1, k1_ref, 0, vb_ref), (0, k2_ref, 0, v2_ref)])
+        run(0, other2, [(1, k1_ref, 0, vb_ref), (0, k2_ref, 0, v2_ref)])
 
     @pl.when(index == 3)
     def _():
-        run(count, other_ref, [(2, k1_ref, 0, vb_ref)])
-
-
-def merge(early_ref, early_stat, late_ref, late_stat, near_ref, far_ref, out_ref):
+        run(0, near3)
+        run(count, other3, [(2, k1_ref, 0, vc_ref)])
+
+
+def merge(early_ref, early_stat, late_ref, late_stat, near_a, near_b, far_ref, out_ref):
     _, width = early_ref.shape
     half = width // 2
     count = half // HEAD_DIM
@@ -428,17 +516,17 @@
 
     @pl.when(index == 1)
     def _():
-        join(0, late_ref, late_stat, near_ref)
-        keep(count, late_ref)
+        join(0, early_ref, early_stat, near_a)
+        keep(count, early_ref)
 
     @pl.when(index == 2)
     def _():
         keep(0, late_ref)
-        join(count, early_ref, early_stat, near_ref)
+        join(count, early_ref, early_stat, near_a)
 
     @pl.when(index == 3)
     def _():
-        join(0, early_ref, early_stat, near_ref)
+        join(0, late_ref, late_stat, near_b)
         join(count, late_ref, late_stat, far_ref)
 
 
@@ -489,7 +577,7 @@
     return ctx == 4 and count % 2 == 0 and count // 2 <= SLOT
 
 
-def shards(streams, short_filter, decay_rate, residue, skip_gain, lengths, queries, keys):
+def in_turn(streams, short_filter, decay_rate, residue, skip_gain, lengths, queries, keys):
     f32, bf16 = jnp.float32, jnp.bfloat16
     shape = jax.ShapeDtypeStruct
     rows, width = streams.shape[1:]
@@ -497,25 +585,75 @@
     modes = decay_rate.shape[1]
     tiles = width // LANES
     ctx = lax.axis_size("ctx")
-    paired = in_pairs(ctx, width)
     halves = shape((rows, half), bf16)
-
-    if paired:
-        rim, q_near, q_far, k_near, k_far = call(
-            pack, (shape((3, SHORT - 1, width), bf16), halves, halves, halves, halves), 3, 0,
-            scratch=[pltpu.VMEM((3, 16, width), bf16), pltpu.SemaphoreType.DMA((5,))],
-            space=HBM,
-        )(*(pltpu.with_memory_space_constraint(a, pltpu.HBM) for a in (streams, queries, keys)))
-        rim = shift(rim, 1)
-        q1 = shift(q_near, -1)
-        q2 = send(q_far, [(3, 1)])
-        k1 = shift(k_near, 1)
-        k2 = send(k_far, [(0, 2)])
-    else:
-        rim = shift(streams[:, rows - SHORT + 1 :, :], 1)
-
     states = (modes * tiles, LANES)
-    gate, long, state, step, block, low, high = call(
+    carried = ((modes + 3 * (SHORT - 1)) * tiles, LANES)
+
+    given = (streams, short_filter, decay_rate.T, residue.T, skip_gain.reshape(tiles, LANES))
+    q_near, q_far, k_near, k_far, *given = call(
+        pack, (halves,) * 4 + tuple(shape(a.shape, a.dtype) for a in given), 2 + len(given), 0,
+        scratch=[pltpu.SemaphoreType.DMA((4 + len(given),))], space=HBM,
+    )(*(pltpu.with_memory_space_constraint(a, pltpu.HBM) for a in (queries, keys, *given)))
+    q2 = send(q_far, [(3, 1)])
+    q1 = shift(q_near, -1)
+    k1 = shift(k_near, 1)
+    k2 = send(k_far, [(0, 2)])
+
+    carry, nears, others = (), [], []
+    for me in range(ctx):
+        last = me == ctx - 1
+        near, other, *after = call(
+            functools.partial(stage, me, last),
+            (halves, halves) + (() if last else (shape(carried, bf16),)),
+            6 + len(carry),
+            scratch=[
+                pltpu.VMEM((rows, width), f32),
+                pltpu.VMEM((rows * tiles, LANES), f32),
+                pltpu.VMEM((rows * tiles, LANES), f32),
+                pltpu.VMEM(states, f32),
+                pltpu.VMEM(states, f32),
+                pltpu.VMEM(carried, f32),
+                pltpu.VMEM((2, 3, SHORT - 1, rows + 16, LANES), f32),
+            ],
+        )(lengths, *given, *carry)
+        carry = [send(a, [(me, me + 1)]) for a in after]
+        nears.append(near)
+        others.append(other)
+    va = send(nears[0], [(0, 1)])
+    v2 = send(others[0], [(0, 2)])
+    vb = send(nears[1], [(1, 2)])
+    vc = send(nears[2], [(2, 3)])
+
+    wide = shape((rows, half + LANES), bf16)
+    o_far = call(hub_far, wide, 6)(lengths, q2, keys, others[1], k1, va)
+    far = send(o_far, [(1, 3)])
+    o_mid = call(hub_mid, wide, 7)(
+        lengths, q1, keys, others[0], others[1], k1, va
+    )
+    near_a = send(o_mid, [(0, 1), (1, 2)])
+    o_last = call(hub_last, wide, 8)(
+        lengths, q1, keys, others[2], k1, vb, k2, v2
+    )
+    near_b = send(o_last, [(2, 3)])
+    means = (shape((rows, width), f32), shape((rows, 2 * LANES), f32))
+    early = call(own_early, means, 10)(lengths, queries, keys, k1, va, *nears[:3], *others[:2])
+    value, *late = call(
+        own_late, (shape((rows, width), bf16), *means), 8 + 2 * ctx
+    )(lengths, queries, keys, k1, vb, vc, k2, v2, *nears, *others)
+    attended = call(merge, shape((rows, width), bf16), 7, 0)(*early, *late, near_a, near_b, far)
+    return value, attended
+
+
+def gathered(streams, short_filter, decay_rate, residue, skip_gain, lengths, queries, keys):
+    f32, bf16 = jnp.float32, jnp.bfloat16
+    shape = jax.ShapeDtypeStruct
+    rows, width = streams.shape[1:]
+    modes = decay_rate.shape[1]
+    tiles = width // LANES
+    ctx = lax.axis_size("ctx")
+    rim = shift(streams[:, rows - SHORT + 1 :, :], 1)
+    states = (modes * tiles, LANES)
+    gate, long, state, step, block = call(
         hyena_local,
         (
             shape((rows, width), f32),
@@ -523,8 +661,6 @@
             shape(states, bf16),
             shape(states, f32),
             shape(states, f32),
-            halves,
-            halves,
         ),
         7,
         scratch=[
@@ -533,51 +669,25 @@
             pltpu.VMEM(states, f32),
         ],
     )(lengths, streams, rim, short_filter, decay_rate.T, residue.T, skip_gain.reshape(tiles, LANES))
-
-    if paired:
-        va = send(high, [(0, 1)])
-        v2 = send(low, [(0, 2)])
-        hops = tuple(range(ctx - 1))
-        parts = [shift(state, hop + 1) for hop in hops]
-    else:
-        every = lax.all_gather(state, "ctx").astype(f32)
-        ends = jnp.cumsum(lengths)
-        before = lax.axis_index("ctx") * rows - 1
-        lasts = (jnp.arange(ctx, dtype=jnp.int32) + 1) * rows - 1
-        same = (lasts <= before) & (
-            doc_of(lasts, ends) == doc_of(jnp.reshape(before, (1,)), ends)
-        )
-        factor = jnp.where(same, (before - lasts) // rows, 0).astype(f32)
-        weight = same.astype(f32)[:, None, None] * block[None] ** factor[:, None, None]
-        parts = [jnp.sum(weight * every, axis=0)]
-        hops = (0,)
-
-    value, *split = call(
-        functools.partial(hyena_cross, hops),
-        (shape((rows, width), bf16),) + ((halves, halves) if paired else ()),
-        5 + len(hops),
+    every = lax.all_gather(state, "ctx").astype(f32)
+    ends = jnp.cumsum(lengths)
+    before = lax.axis_index("ctx") * rows - 1
+    lasts = (jnp.arange(ctx, dtype=jnp.int32) + 1) * rows - 1
+    same = (lasts <= before) & (doc_of(lasts, ends) == doc_of(jnp.reshape(before, (1,)), ends))
+    factor = jnp.where(same, (before - lasts) // rows, 0).astype(f32)
+    weight = same.astype(f32)[:, None, None] * block[None] ** factor[:, None, None]
+    value = call(
+        functools.partial(hyena_cross, (0,)),
+        shape((rows, width), bf16),
+        6,
         scratch=[pltpu.VMEM((rows * tiles, LANES), f32)],
-    )(lengths, step, block, long, gate, *parts)
-
-    if not paired:
-        return value, gathered_attention(lengths, queries, keys, value)
-
-    near, other = split
-    vb = send(near, [(1, 2), (2, 3)])
-    wide = shape((rows, half + LANES), bf16)
-    o_far = call(hub_far, wide, 6)(lengths, q2, keys, other, k1, va)
-    far = send(o_far, [(1, 3)])
-    means = (shape((rows, width), f32), shape((rows, 2 * LANES), f32))
-    early = call(own_early, means, 5)(lengths, queries, keys, near, other)
-    o_near = call(hub_near, wide, 9)(
-        lengths, q1, keys, other, k1, va, vb, k2, v2
-    )
-    last = shift(o_near, 1)
-    late = call(own_late, means, 10)(lengths, queries, keys, near, other, k1, va, vb, k2, v2)
-    attended = call(merge, shape((rows, width), bf16), 6, 0)(
-        *early, *late, last, far
-    )
-    return value, attended
+    )(lengths, step, block, long, gate, jnp.sum(weight * every, axis=0))
+    return value, gathered_attention(lengths, queries, keys, value)
+
+
+def shards(streams, *rest):
+    plan = in_turn if in_pairs(lax.axis_size("ctx"), streams.shape[2]) else gathered
+    return plan(streams, *rest)
 
 
 def solution(mesh):

time: 67.4 us -> 90 us (1.34)
  the two profiles are of different devices: /device:TPU:0 before, /device:TPU:30 now
where the time goes in v1:
time: 90 us; the launch traced here: 89.7 us
  starting transfers between devices  36.5 us (41%)
  waiting for transfers between devices  34.5 us (38%)
  Pallas kernels  17.7 us (20%)
  between operations  0.94 us (1%)
    ppermute x14, starting transfers between devices, send(): return lax.ppermute(value, 'ctx', pairs)  36.5 us
    ppermute x14, waiting for transfers between devices, send(): return lax.ppermute(value, 'ctx', pairs)  34.5 us
    pallas_call x4, Pallas kernels, in_turn(): call(functools.partial(stage, me, last), (halves, halves) + (() if last e...  7.26 us
    pallas_call x1, Pallas kernels, in_turn(): call(own_late, (shape((rows, width), bf16), *means), 8 + 2 * ctx)  4.27 us
    pallas_call x1, Pallas kernels, in_turn(): call(merge, shape((rows, width), bf16), 7, 0)  1.87 us
    pallas_call x1, Pallas kernels, in_turn(): call(pack, (halves,) * 4 + tuple((shape(a.shape, a.dtype) for a in given)...  1.87 us
  transfers between devices with their start and end apart: 14, of which 2 were waited for; matrix products, arithmetic and copies ran while one was open for 0% of the time, Pallas kernels for 16%

profile of v1, /device:TPU:30, one launch (start us, length us, event | category | flops | bytes accessed | tf_op | source)
XLA Modules:
  0.0 89.7 jit_solution(9036532584831119081)
XLA Ops:
  0.6 1.9 %shard_map.95 = (bf16[128,1024]{1,0:T(8,128)(2,1)S(1)}, bf16[128,1024]{1,0:T(8,128)(2,1)S(1)}, bf16[128,1024]{1,0:T(8,128)(2,1)S(1)}, bf16[128,1024]{1,0:T(8,128...) custom-call(bf16[128,2048]{1,0:T(8,128)(2,1)} %query_ref.3, ...), custom_call_target="tpu_custom_call" | custom-call | flops 10000000 | bytes 4000000 | tf_op jit(solution)/shard_map/pallas_call | solution.py:593
  2.5 1.3 %collective-permute-start = (bf16[128,1024]{1,0:T(8,128)(2,1)S(1)}, bf16[128,1024]{1,0:T(8,128)(2,1)S(1)}, u32[]{:S(2)}, u32[]{:S(2)}) collective-permute-start(bf16[128,1024]{1,0:T(8,128)(2,1)S(1)} %get-tuple-element.27), channel_id=1, source_target_pairs={{0,4},{4,8},{8,12},{1,5},{5,9},{9,13},{2,6},{6,10},{10,14},{3,7},{... | collective-permute-start | bytes 786440 | tf_op jit(solution)/shard_map/ppermute | solution.py:567
  4.4 0.7 collective-permute-start.8
  5.1 0.8 collective-permute-start.1
  6.5 0.7 collective-permute-start.3
  7.1 5.2 %collective-permute-start.9 = (bf16[128,1024]{1,0:T(8,128)(2,1)S(1)}, bf16[128,1024]{1,0:T(8,128)(2,1)S(1)}, u32[]{:S(2)}, u32[]{:S(2)}) collective-permute-start(bf16[128,1024]{1,0:T(8,128)(2,1)S(1)} %get-tuple-element.50), channel_id=1, source_target_pairs={{4,0},{8,4},{12,8},{5,1},{9,5},{13,9},{6,2},{10,6},{14,10},{7,3},{... | collective-permute-start | bytes 786440 | tf_op jit(solution)/shard_map/ppermute | solution.py:567
  12.3 19.9 %collective-permute-start.12 = (bf16[128,1024]{1,0:T(8,128)(2,1)S(1)}, bf16[128,1024]{1,0:T(8,128)(2,1)S(1)}, u32[]{:S(2)}, u32[]{:S(2)}) collective-permute-start(bf16[128,1024]{1,0:T(8,128)(2,1)S(1)} %get-tuple-element.51), channel_id=1, source_target_pairs={{12,4},{13,5},{14,6},{15,7},{28,20},{29,21},{30,22},{31,23}} | collective-permute-start | bytes 786440 | tf_op jit(solution)/shard_map/ppermute | solution.py:567
  32.3 0.7 collective-permute-start.5
  33.0 0.7 collective-permute-start.6
  33.7 0.7 collective-permute-start.2
  34.3 0.6 shard_map.98
  34.9 0.6 shard_map.102
  35.5 0.7 collective-permute-start.10
  36.2 0.8 collective-permute-done.12.q2_ref
  37.5 1.4 %collective-permute-start.13 = (bf16[128,1152]{1,0:T(8,128)(2,1)S(1)}, bf16[128,1152]{1,0:T(8,128)(2,1)S(1)}, u32[]{:S(2)}, u32[]{:S(2)}) collective-permute-start(bf16[128,1152]{1,0:T(8,128)(2,1)S(1)} %shard_map.104), channel_id=1, source_target_pairs={{4,12},{5,13},{6,14},{7,15},{20,28},{21,29},{22,30},{23,31}} | collective-permute-start | bytes 884744 | tf_op jit(solution)/shard_map/ppermute | solution.py:567
  39.0 0.7 shard_map.103
  39.8 1.3 %collective-permute-start.11 = (bf16[128,1152]{1,0:T(8,128)(2,1)S(1)}, bf16[128,1152]{1,0:T(8,128)(2,1)S(1)}, u32[]{:S(2)}, u32[]{:S(2)}) collective-permute-start(bf16[128,1152]{1,0:T(8,128)(2,1)S(1)} %shard_map.103), channel_id=1, source_target_pairs={{8,12},{9,13},{10,14},{11,15},{24,28},{25,29},{26,30},{27,31}} | collective-permute-start | bytes 884744 | tf_op jit(solution)/shard_map/ppermute | solution.py:567
  41.1 1.3 %collective-permute-start.4 = (bf16[128,1024]{1,0:T(8,128)(2,1)S(1)}, bf16[128,1024]{1,0:T(8,128)(2,1)S(1)}, u32[]{:S(2)}, u32[]{:S(2)}) collective-permute-start(bf16[128,1024]{1,0:T(8,128)(2,1)S(1)} %get-tuple-element.36.near2), channel_id=1, source_target_pairs={{8,12},{9,13},{10,14},{11,15},{24,28},{25,29},{26,30},{27,31}} | collective-permute-start | bytes 786440 | tf_op jit(solution)/shard_map/ppermute | solution.py:567
  42.4 1.3 %collective-permute-start.7 = (bf16[352,128]{1,0:T(8,128)(2,1)S(1)}, bf16[352,128]{1,0:T(8,128)(2,1)S(1)}, u32[]{:S(2)}, u32[]{:S(2)}) collective-permute-start(bf16[352,128]{1,0:T(8,128)(2,1)S(1)} %get-tuple-element.40), channel_id=1, source_target_pairs={{8,12},{9,13},{10,14},{11,15},{24,28},{25,29},{26,30},{27,31}} | collective-permute-start | bytes 270344 | tf_op jit(solution)/shard_map/ppermute | solution.py:567
  43.7 0.6 shard_map.101
  44.2 33.7 %collective-permute-done.7.refs_0_ = bf16[352,128]{1,0:T(8,128)(2,1)S(1)} collective-permute-done((bf16[352,128]{1,0:T(8,128)(2,1)S(1)}, bf16[352,128]{1,0:T(8,128)(2,1)S(1)}, u32[]{:S(2)}, u32[]{:S(2)}) %collective-permute-start.7) | collective-permute-done | bytes 90144 | tf_op jit(solution)/shard_map/ppermute | solution.py:567
  77.9 5.6 %shard_map.99 = (bf16[128,1024]{1,0:T(8,128)(2,1)S(1)}, bf16[128,1024]{1,0:T(8,128)(2,1)S(1)}) custom-call(s32[2]{0:T(128)S(1)} %copy-done.2, bf16[3,128,2048]{2,1,0:T(8,128)(2,1)S(1)} %get-tuple-element.28.streams_ref, f32[3,3,2048]{2,1,0:T(4,128)S(1)} %get-tuple-element.29.taps_ref, f32[16,2048]{1,0:T(8,128)S(1)} %get-tuple-element.30.decay_ref, ...), custom_call_target="tpu_custom_call" | custom-call | flops 10000000 | bytes 4000000 | tf_op jit(solution)/shard_map/pallas_call | solution.py:605
  83.5 4.3 %shard_map.100 = (bf16[128,2048]{1,0:T(8,128)(2,1)}, f32[128,2048]{1,0:T(8,128)S(1)}, f32[128,256]{1,0:T(8,128)S(1)}) custom-call(s32[2]{0:T(128)S(1)} %copy-done.2, bf16[128,2048]{1,0:T(8,128)(2,1)S(1)} %copy-done.1, bf16[128,2048]{1,0:T(8,128)(2,1)S(1)} %copy-done, bf16[128,1024]{1,0:T(8,128)(2,1)S(1)} %collective-permute-done.k1_ref, ...), custom_call_target="tpu_custom_call" | custom-call | flops 10000000 | bytes 4000000 | tf_op jit(solution)/shard_map/pallas_call | solution.py:640
  87.8 1.9 %shard_map.105 = bf16[128,2048]{1,0:T(8,128)(2,1)} custom-call(f32[128,2048]{1,0:T(8,128)S(1)} %get-tuple-element.46.early_ref, f32[128,256]{1,0:T(8,128)S(1)} %get-tuple-element.47.early_stat, f32[128,2048]{1,0:T(8,128)S(1)} %get-tuple-element.48.late_ref, f32[128,256]{1,0:T(8,128)S(1)} %get-tuple-element.49.late_stat, ...), custom_call_target="tpu_custom_call" | custom-call | flops 10000000 | bytes 4000000 | tf_op jit(solution)/shard_map/pallas_call | solution.py:643
  (21 shorter events, 1.7 us)
Async XLA Ops:
  0.6 3.2 %copy-start.2 = (s32[2]{0:T(128)S(1)}, s32[2]{0:T(128)}, u32[]{:S(2)}) copy-start(s32[2]{0:T(128)} %lengths_ref.17) | copy-start | bytes 28
  2.5 30.4 %collective-permute-start = (bf16[128,1024]{1,0:T(8,128)(2,1)S(1)}, bf16[128,1024]{1,0:T(8,128)(2,1)S(1)}, u32[]{:S(2)}, u32[]{:S(2)}) collective-permute-start(bf16[128,1024]{1,0:T(8,128)(2,1)S(1)} %get-tuple-element.27), channel_id=1, source_target_pairs={{0,4},{4,8},{8,12},{1,5},{5,9},{9,13},{2,6},{6,10},{10,14},{3,7},{... | collective-permute-start | bytes 786440 | tf_op jit(solution)/shard_map/ppermute | solution.py:567
  4.4 29.3 %collective-permute-start.8 = (bf16[128,1024]{1,0:T(8,128)(2,1)S(1)}, bf16[128,1024]{1,0:T(8,128)(2,1)S(1)}, u32[]{:S(2)}, u32[]{:S(2)}) collective-permute-start(bf16[128,1024]{1,0:T(8,128)(2,1)S(1)} %get-tuple-element.39.near0), channel_id=1, source_target_pairs={{0,4},{1,5},{2,6},{3,7},{16,20},{17,21},{18,22},{19,23}} | collective-permute-start | bytes 786440 | tf_op jit(solution)/shard_map/ppermute | solution.py:567
  5.1 29.8 %copy-start = (bf16[128,2048]{1,0:T(8,128)(2,1)S(1)}, bf16[128,2048]{1,0:T(8,128)(2,1)}, u32[]{:S(2)}) copy-start(bf16[128,2048]{1,0:T(8,128)(2,1)} %key_ref.9) | copy-start | bytes 1572868
  5.1 0.8 collective-permute-start.1
  6.5 25.8 %collective-permute-start.3 = (bf16[352,128]{1,0:T(8,128)(2,1)S(1)}, bf16[352,128]{1,0:T(8,128)(2,1)S(1)}, u32[]{:S(2)}, u32[]{:S(2)}) collective-permute-start(bf16[352,128]{1,0:T(8,128)(2,1)S(1)} %get-tuple-element.35), channel_id=1, source_target_pairs={{4,8},{5,9},{6,10},{7,11},{20,24},{21,25},{22,26},{23,27}} | collective-permute-start | bytes 270344 | tf_op jit(solution)/shard_map/ppermute | solution.py:567
  7.1 27.8 %collective-permute-start.9 = (bf16[128,1024]{1,0:T(8,128)(2,1)S(1)}, bf16[128,1024]{1,0:T(8,128)(2,1)S(1)}, u32[]{:S(2)}, u32[]{:S(2)}) collective-permute-start(bf16[128,1024]{1,0:T(8,128)(2,1)S(1)} %get-tuple-element.50), channel_id=1, source_target_pairs={{4,0},{8,4},{12,8},{5,1},{9,5},{13,9},{6,2},{10,6},{14,10},{7,3},{... | collective-permute-start | bytes 786440 | tf_op jit(solution)/shard_map/ppermute | solution.py:567
  12.3 24.6 %collective-permute-start.12 = (bf16[128,1024]{1,0:T(8,128)(2,1)S(1)}, bf16[128,1024]{1,0:T(8,128)(2,1)S(1)}, u32[]{:S(2)}, u32[]{:S(2)}) collective-permute-start(bf16[128,1024]{1,0:T(8,128)(2,1)S(1)} %get-tuple-element.51), channel_id=1, source_target_pairs={{12,4},{13,5},{14,6},{15,7},{28,20},{29,21},{30,22},{31,23}} | collective-permute-start | bytes 786440 | tf_op jit(solution)/shard_map/ppermute | solution.py:567
  32.3 6.7 %collective-permute-start.5 = (bf16[128,1024]{1,0:T(8,128)(2,1)S(1)}, bf16[128,1024]{1,0:T(8,128)(2,1)S(1)}, u32[]{:S(2)}, u32[]{:S(2)}) collective-permute-start(bf16[128,1024]{1,0:T(8,128)(2,1)S(1)} %get-tuple-element.37), channel_id=1, source_target_pairs={{0,8},{1,9},{2,10},{3,11},{16,24},{17,25},{18,26},{19,27}} | collective-permute-start | bytes 786440 | tf_op jit(solution)/shard_map/ppermute | solution.py:567
  33.0 6.0 %collective-permute-start.6 = (bf16[128,1024]{1,0:T(8,128)(2,1)S(1)}, bf16[128,1024]{1,0:T(8,128)(2,1)S(1)}, u32[]{:S(2)}, u32[]{:S(2)}) collective-permute-start(bf16[128,1024]{1,0:T(8,128)(2,1)S(1)} %get-tuple-element.38.other0), channel_id=1, source_target_pairs={{0,8},{1,9},{2,10},{3,11},{16,24},{17,25},{18,26},{19,27}} | collective-permute-start | bytes 786440 | tf_op jit(solution)/shard_map/ppermute | solution.py:567
  33.7 5.3 %collective-permute-start.2 = (bf16[128,1024]{1,0:T(8,128)(2,1)S(1)}, bf16[128,1024]{1,0:T(8,128)(2,1)S(1)}, u32[]{:S(2)}, u32[]{:S(2)}) collective-permute-start(bf16[128,1024]{1,0:T(8,128)(2,1)S(1)} %get-tuple-element.34.near1), channel_id=1, source_target_pairs={{4,8},{5,9},{6,10},{7,11},{20,24},{21,25},{22,26},{23,27}} | collective-permute-start | bytes 786440 | tf_op jit(solution)/shard_map/ppermute | solution.py:567
  35.5 52.3 %collective-permute-start.10 = (bf16[128,1152]{1,0:T(8,128)(2,1)S(1)}, bf16[128,1152]{1,0:T(8,128)(2,1)S(1)}, u32[]{:S(2)}, u32[]{:S(2)}) collective-permute-start(bf16[128,1152]{1,0:T(8,128)(2,1)S(1)} %shard_map.102), channel_id=1, source_target_pairs={{0,4},{4,8},{1,5},{5,9},{2,6},{6,10},{3,7},{7,11},{16,20},{20,24},... | collective-permute-start | bytes 884744 | tf_op jit(solution)/shard_map/ppermute | solution.py:567
  37.5 6.1 %copy-start.1 = (bf16[128,2048]{1,0:T(8,128)(2,1)S(1)}, bf16[128,2048]{1,0:T(8,128)(2,1)}, u32[]{:S(2)}) copy-start(bf16[128,2048]{1,0:T(8,128)(2,1)} %query_ref.3) | copy-start | bytes 1572868
  37.5 50.3 %collective-permute-start.13 = (bf16[128,1152]{1,0:T(8,128)(2,1)S(1)}, bf16[128,1152]{1,0:T(8,128)(2,1)S(1)}, u32[]{:S(2)}, u32[]{:S(2)}) collective-permute-start(bf16[128,1152]{1,0:T(8,128)(2,1)S(1)} %shard_map.104), channel_id=1, source_target_pairs={{4,12},{5,13},{6,14},{7,15},{20,28},{21,29},{22,30},{23,31}} | collective-permute-start | bytes 884744 | tf_op jit(solution)/shard_map/ppermute | solution.py:567
  39.8 48.1 %collective-permute-start.11 = (bf16[128,1152]{1,0:T(8,128)(2,1)S(1)}, bf16[128,1152]{1,0:T(8,128)(2,1)S(1)}, u32[]{:S(2)}, u32[]{:S(2)}) collective-permute-start(bf16[128,1152]{1,0:T(8,128)(2,1)S(1)} %shard_map.103), channel_id=1, source_target_pairs={{8,12},{9,13},{10,14},{11,15},{24,28},{25,29},{26,30},{27,31}} | collective-permute-start | bytes 884744 | tf_op jit(solution)/shard_map/ppermute | solution.py:567
  41.1 42.5 %collective-permute-start.4 = (bf16[128,1024]{1,0:T(8,128)(2,1)S(1)}, bf16[128,1024]{1,0:T(8,128)(2,1)S(1)}, u32[]{:S(2)}, u32[]{:S(2)}) collective-permute-start(bf16[128,1024]{1,0:T(8,128)(2,1)S(1)} %get-tuple-element.36.near2), channel_id=1, source_target_pairs={{8,12},{9,13},{10,14},{11,15},{24,28},{25,29},{26,30},{27,31}} | collective-permute-start | bytes 786440 | tf_op jit(solution)/shard_map/ppermute | solution.py:567
  42.4 35.6 %collective-permute-start.7 = (bf16[352,128]{1,0:T(8,128)(2,1)S(1)}, bf16[352,128]{1,0:T(8,128)(2,1)S(1)}, u32[]{:S(2)}, u32[]{:S(2)}) collective-permute-start(bf16[352,128]{1,0:T(8,128)(2,1)S(1)} %get-tuple-element.40), channel_id=1, source_target_pairs={{8,12},{9,13},{10,14},{11,15},{24,28},{25,29},{26,30},{27,31}} | collective-permute-start | bytes 270344 | tf_op jit(solution)/shard_map/ppermute | solution.py:567
